TPU v7x, 512 devices: a whole 4x4x16 slice. The times are simulated.
512 devices in a mesh: dp: 32 (over z_lo, x), tensor: 16 (over z_hi, y, core).
Axes of the slice: x: 4, y: 4, z: 16 (z_hi: 2, z_lo: 8; z = z_hi * 8 + z_lo), core: 2. Of those that a mesh axis runs over, the one named last changes fastest.
Arguments:
- out_grad: bfloat16 [4096, 4096], P(('dp', 'tensor')), may hold values from -6 to 6
- gate_pre: bfloat16 [4096, 14336], P('dp', 'tensor'), may hold values from -6 to 6
- up_pre: bfloat16 [4096, 14336], P('dp', 'tensor'), may hold values from -6 to 6
- down_weight: bfloat16 [14336, 4096], P('tensor', 'dp'), may hold values from -6 to 6
- moment: float32 [14336, 4096], P('tensor', 'dp'), may hold values from -4 to 4
- second: float32 [14336, 4096], P('tensor', 'dp'), may hold values from 0.01 to 0.5
- decay_mask: int32 [14336], P('tensor'), may hold values 0 or 1
Outputs:
- grad_gate: bfloat16 [4096, 14336], P('dp', 'tensor')
- grad_up: bfloat16 [4096, 14336], P('dp', 'tensor')
- new_weight: bfloat16 [14336, 4096], P('tensor', 'dp')
- new_moment: float32 [14336, 4096], P('tensor', 'dp')
- new_second: float32 [14336, 4096], P('tensor', 'dp')
All inputs are finite; a program needn't handle non-finite values. No bound on the sum of `decay_mask` on one device may be relied on, other than what follows from the above.
Results may differ from a plain program's by a relative error of at most 0.0014.
Values may be sent and summed in bfloat16 or wider, within the bound.
A program may use at most 64 MiB of HBM per device.

v0:
```python
import math
import jax
import jax.numpy as jnp
from jax import lax
from jax.sharding import Mesh
from jax.sharding import PartitionSpec as P

FF = 14336
OPT_STEP = 10
BETA_ONE = 0.9
BETA_TWO = 0.95
LEARN_RATE = 0.1
DECAY_RATE = 0.5
ADAM_EPS = 1e-08
DP = ("zl", "x")
TP = ("zh", "y", "c")


def body(out_grad, gate_pre, up_pre, down_weight, moment, second, decay_mask):
    factor = 1.0 / math.sqrt(FF)
    group_grad = lax.all_gather(out_grad, "c", axis=0, tiled=True)
    group_grad = lax.all_gather(group_grad, "y", axis=0, tiled=True)
    group_grad = lax.all_gather(group_grad, "zh", axis=0, tiled=True)
    gate = gate_pre.astype(jnp.float32)
    up = up_pre.astype(jnp.float32)
    sigmoid_gate = jax.nn.sigmoid(gate)
    activated = gate * sigmoid_gate
    hidden = (activated * up).astype(jnp.bfloat16)
    columns = lax.all_to_all(group_grad, DP, split_axis=1, concat_axis=0, tiled=True)
    stacked = jnp.stack([down_weight, hidden.T])
    stacked = lax.all_gather(stacked, "x", axis=2, tiled=True)
    stacked = lax.all_gather(stacked, "zl", axis=2, tiled=True)
    back_sum = lax.dot_general(
        group_grad, stacked[0], (((1,), (1,)), ((), ())), preferred_element_type=jnp.float32
    )
    grad_sum = lax.dot_general(
        stacked[1], columns, (((1,), (0,)), ((), ())), preferred_element_type=jnp.float32
    )
    back = back_sum * factor
    grad_up = (back * activated).astype(jnp.bfloat16)
    grad_gate = (back * up * sigmoid_gate * (1.0 + gate * (1.0 - sigmoid_gate))).astype(
        jnp.bfloat16
    )
    weight_grad = grad_sum * factor
    new_moment = BETA_ONE * moment + (1.0 - BETA_ONE) * weight_grad
    new_second = BETA_TWO * second + (1.0 - BETA_TWO) * weight_grad * weight_grad
    fix_one = 1.0 - BETA_ONE**OPT_STEP
    fix_two = 1.0 - BETA_TWO**OPT_STEP
    weight = down_weight.astype(jnp.float32)
    decay = decay_mask.astype(jnp.float32)[:, None]
    direction = (
        new_moment / fix_one / (jnp.sqrt(new_second / fix_two) + ADAM_EPS)
        + DECAY_RATE * decay * weight
    )
    new_weight = (weight - LEARN_RATE * direction).astype(jnp.bfloat16)
    return (grad_gate, grad_up, new_weight, new_moment, new_second)


def solution(mesh):
    zl, x = (8, mesh.shape["dp"] // 8)
    zh = mesh.shape["tensor"] // 8
    fine = Mesh(mesh.devices.reshape(zl, x, zh, 4, 2), DP + TP)
    return jax.shard_map(
        body,
        mesh=fine,
        in_specs=(P(DP + TP, None), P(DP, TP), P(DP, TP), P(TP, DP), P(TP, DP), P(TP, DP), P(TP)),
        out_specs=(P(DP, TP), P(DP, TP), P(TP, DP), P(TP, DP), P(TP, DP)),
        check_vma=False,
    )
```

profile of v0, /device:TPU:105, one launch (start us, length us, event | category | flops | bytes accessed | tf_op | source)
XLA Modules:
  0.0 484.9 jit_solution(10351806163342086163)
XLA Ops:
  7.2 0.0 all-gather.4.cloned.1.call-start
  7.2 1.1 copy.26
  8.3 1.1 copy.27
  9.4 0.1 fusion.15
  9.6 0.0 copy-start
  9.6 0.0 copy-start.1
  9.6 1.8 pad_maximum_fusion
  11.4 0.0 all-gather.4.cloned.1.call-update
  11.4 0.0 all-gather.8.cloned.1.call-start
  11.5 2.4 all_gather.17
  13.9 10.8 %all_gather.18 = bf16[64,4096]{1,0:T(8,128)(2,1)} all-gather(bf16[16,4096]{1,0:T(8,128)(2,1)S(1)} %all_gather.17), channel_id=1, replica_groups=mesh['zl'=8,'x'=4,'zh'=2,'y'=4,'c'=2] {'y'}, dimensions={0}, use_global_device_ids=true | all-gather | bytes 655360 | tf_op jit(solution)/shard_map/all_gather | solution.py:22
  24.8 0.0 all-gather.8.cloned.1.call-update
  24.8 0.0 all-gather.6.cloned.1.call-start
  24.9 29.2 %all-gather.4.cloned.1.call-done = bf16[2,896,512]{2,1,0:T(8,128)(2,1)} async-done(((bf16[2,896,128]{2,1,0:T(8,128)(2,1)}), bf16[2,896,512]{2,1,0:T(8,128)(2,1)}) %all-gather.4.cloned.1.call-update) | async-done | bytes 1835024 | tf_op jit(solution)/shard_map/all_gather | solution.py:31
  54.0 0.0 all-gather.6.cloned.1.call-update
  54.0 76.9 %all-gather.8.cloned.1.call-done = bf16[128,4096]{1,0:T(8,128)(2,1)} async-done(((bf16[64,4096]{1,0:T(8,128)(2,1)}), bf16[128,4096]{1,0:T(8,128)(2,1)}) %all-gather.8.cloned.1.call-update) | async-done | bytes 1048592 | tf_op jit(solution)/shard_map/all_gather | solution.py:23
  131.0 2.3 copy.28
  133.3 7.1 %all-to-all-start = ((bf16[128,32,128]{0,2,1:T(8,128)(2,1)}), bf16[128,32,128]{0,2,1:T(8,128)(2,1)S(1)}, u32[]{:S(2)}, u32[]{:S(2)}) async-start(bf16[128,32,128]{0,2,1:T(8,128)(2,1)} %bitcast.6), calls=%async_computation | async-start | bytes 2097152 | tf_op jit(solution)/shard_map/all_to_all | solution.py:29
  140.4 0.7 convert_multiply_fusion.5
  141.1 92.0 %all-to-all-done = bf16[128,32,128]{0,2,1:T(8,128)(2,1)S(1)} async-done(((bf16[128,32,128]{0,2,1:T(8,128)(2,1)}), bf16[128,32,128]{0,2,1:T(8,128)(2,1)S(1)}, u32[]{:S(2)}, u32[]{:S(2)}) %all-to-all-start) | async-done | bytes 1048608 | tf_op jit(solution)/shard_map/all_to_all | solution.py:29
  233.1 0.7 copy.29
  233.8 0.0 copy-start.2
  233.8 231.0 %all-gather.6.cloned.1.call-done = bf16[2,896,4096]{2,1,0:T(8,128)(2,1)} async-done(((bf16[2,896,512]{2,1,0:T(8,128)(2,1)}), bf16[2,896,4096]{2,1,0:T(8,128)(2,1)}) %all-gather.6.cloned.1.call-update) | async-done | bytes 14680080 | tf_op jit(solution)/shard_map/all_gather | solution.py:32
  464.9 5.4 %multiply_convert_fusion = (bf16[128,896]{0,1:T(8,128)(2,1)S(1)}, bf16[128,896]{0,1:T(8,128)(2,1)S(1)}) fusion(bf16[128,896]{0,1:T(8,128)(2,1)S(1)} %copy.26, bf16[128,896]{0,1:T(8,128)(2,1)S(1)} %copy.27, bf16[128,4096]{1,0:T(8,128)(2,1)} %all-gather.8.cloned.1.call-done, bf16[2,896,4096]{2,1,0:T(8,128)(2,1)} %all-gather.6.cloned.1.call-done), kind=kOutput, calls=%fused_computation.27 | convolution fusion | flops 941359104 | bytes 9306112 | tf_op jit(solution)/shard_map/dot_general | solution.py:33
  470.3 0.8 copy.31
  471.2 0.8 copy.30
  472.0 0.0 copy-done
  472.0 0.0 copy-done.1
  472.0 0.0 copy-done.2
  472.0 6.4 %fusion.10 = (bf16[896,128]{1,0:T(8,128)(2,1)}, f32[896,128]{1,0:T(8,128)}, f32[896,128]{1,0:T(8,128)}) fusion(bf16[896,128]{1,0:T(8,128)(2,1)S(1)} %copy-done, f32[896]{0:T(1024)S(1)} %convert_multiply_fusion.5, f32[896,128]{1,0:T(8,128)S(1)} %copy-done.1, f32[896,128]{1,0:T(8,128)S(1)} %copy-done.2, bf16[4096,128]{1,0:T(8,128)(2,1)S(1)} %bitcast.27, ...), kind=kOutput, calls=%fused_computation.19 | convolution fusion | flops 941588480 | bytes 10685952 | tf_op jit(solution)/shard_map/dot_general | solution.py:36
Async XLA Ops:
  7.2 46.8 %all-gather.4.cloned.1.call-start = ((), (), s32[]{:S(2)}) async-start(), calls=%async_computation.1 | async-start | bytes 2293760 | tf_op jit(solution)/shard_map/all_gather | solution.py:31
  9.6 462.4 %copy-start = (bf16[896,128]{1,0:T(8,128)(2,1)S(1)}, bf16[896,128]{1,0:T(8,128)(2,1)}, u32[]{:S(2)}) copy-start(bf16[896,128]{1,0:T(8,128)(2,1)} %param.10) | copy-start | bytes 688132
  9.6 462.4 %copy-start.1 = (f32[896,128]{1,0:T(8,128)S(1)}, f32[896,128]{1,0:T(8,128)}, u32[]{:S(2)}) copy-start(f32[896,128]{1,0:T(8,128)} %param.11) | copy-start | bytes 1376260
  11.4 119.5 %all-gather.8.cloned.1.call-start = ((), (), s32[]{:S(2)}) async-start(), calls=%async_computation.3 | async-start | bytes 1572864 | tf_op jit(solution)/shard_map/all_gather | solution.py:23
  24.8 440.1 %all-gather.6.cloned.1.call-start = ((), (), s32[]{:S(2)}) async-start(), calls=%async_computation.2 | async-start | bytes 16515072 | tf_op jit(solution)/shard_map/all_gather | solution.py:32
  133.3 99.9 %all-to-all-start = ((bf16[128,32,128]{0,2,1:T(8,128)(2,1)}), bf16[128,32,128]{0,2,1:T(8,128)(2,1)S(1)}, u32[]{:S(2)}, u32[]{:S(2)}) async-start(bf16[128,32,128]{0,2,1:T(8,128)(2,1)} %bitcast.6), calls=%async_computation | async-start | bytes 2097152 | tf_op jit(solution)/shard_map/all_to_all | solution.py:29
  233.8 238.2 %copy-start.2 = (f32[896,128]{1,0:T(8,128)S(1)}, f32[896,128]{1,0:T(8,128)}, u32[]{:S(2)}) copy-start(f32[896,128]{1,0:T(8,128)} %param.12) | copy-start | bytes 1376260
Sparse Core Ops, SparseCore 0:
  11.6 42.3 all-gather.3
  56.1 74.8 all-gather.7
  133.1 331.7 all-gather.5
where the time goes:
time: 485 us
  waiting for transfers between devices  429 us (88%)
  between operations  13.8 us (3%)
  blocking collectives  13.3 us (3%)
  matrix products  11.8 us (2%)
  starting transfers between devices  7.26 us (1%)
  local copies, waits for them, and re-layouts  6.87 us (1%)
    all_gather x1, waiting for transfers between devices, body(): stacked = lax.all_gather(stacked, 'zl', axis=2, tiled=True)  231 us
    all_to_all x1, waiting for transfers between devices, body(): lax.all_to_all(group_grad, DP, split_axis=1, concat_axis=0, tiled=True)  92 us
    all_gather x1, waiting for transfers between devices, body(): group_grad = lax.all_gather(group_grad, 'zh', axis=0, tiled=True)  76.9 us
    all_gather x1, waiting for transfers between devices, body(): stacked = lax.all_gather(stacked, 'x', axis=2, tiled=True)  29.2 us
    all_gather x1, blocking collectives, body(): group_grad = lax.all_gather(group_grad, 'y', axis=0, tiled=True)  10.8 us
  transfers between devices with their start and end apart: 4, of which 4 were waited for; matrix products, arithmetic and copies ran while one was open for 1% of the time, Pallas kernels for 0%

commit v1 on v0

--- a/solution.py
+++ b/solution.py
@@ -28,7 +28,10 @@
     hidden = (activated * up).astype(jnp.bfloat16)
     columns = lax.all_to_all(group_grad, DP, split_axis=1, concat_axis=0, tiled=True)
     stacked = jnp.stack([down_weight, hidden.T])
-    stacked = lax.all_gather(stacked, "x", axis=2, tiled=True)
+    n_dev = lax.axis_size("x")
+    blocks = jnp.stack([stacked for _ in range(n_dev)])
+    blocks = lax.all_to_all(blocks, "x", split_axis=0, concat_axis=0)
+    stacked = jnp.concatenate(blocks, axis=2)
     stacked = lax.all_gather(stacked, "zl", axis=2, tiled=True)
     back_sum = lax.dot_general(
         group_grad, stacked[0], (((1,), (1,)), ((), ())), preferred_element_type=jnp.float32

time: 485 us -> 464 us (0.957)
  waiting for transfers between devices: 429 us -> 401 us
    all_gather x1 -> x0, waiting for transfers between devices: 29.2 us -> none  [body(): stacked = lax.all_gather(stacked, 'x', axis=2, tiled=True)]
    all_to_all x0 -> x1, waiting for transfers between devices: none -> 8.61 us  [body(): blocks = lax.all_to_all(blocks, 'x', split_axis=0, concat_axis=0)]
    all_gather x1, waiting for transfers between devices: 76.9 us -> 68.8 us  [body(): group_grad = lax.all_gather(group_grad, 'zh', axis=0, tiled=True)]
where the time goes in v1:
time: 464 us
  waiting for transfers between devices  401 us (86%)
  between operations  14.1 us (3%)
  blocking collectives  13.9 us (3%)
  matrix products  11.9 us (3%)
  starting transfers between devices  11.3 us (2%)
  local copies, waits for them, and re-layouts  10.1 us (2%)
    all_gather x1, waiting for transfers between devices, body(): stacked = lax.all_gather(stacked, 'zl', axis=2, tiled=True)  231 us
    all_to_all x1, waiting for transfers between devices, body(): lax.all_to_all(group_grad, DP, split_axis=1, concat_axis=0, tiled=True)  92.7 us
    all_gather x1, waiting for transfers between devices, body(): group_grad = lax.all_gather(group_grad, 'zh', axis=0, tiled=True)  68.8 us
    all_gather x1, blocking collectives, body(): group_grad = lax.all_gather(group_grad, 'y', axis=0, tiled=True)  11.4 us
  transfers between devices with their start and end apart: 4, of which 4 were waited for; matrix products, arithmetic and copies ran while one was open for 1% of the time, Pallas kernels for 0%

profile of v1, /device:TPU:105, one launch (start us, length us, event | category | flops | bytes accessed | tf_op | source)
XLA Modules:
  0.0 463.6 jit_solution(8240255189773664259)
XLA Ops:
  7.2 0.0 copy-start.1
  7.2 1.1 copy.28
  8.3 1.1 copy.29
  9.4 0.1 fusion.15
  9.6 1.0 pad_maximum_fusion
  10.6 0.3 copy.30
  10.8 1.5 stack.19
  12.3 0.0 copy-start.2
  12.3 4.1 all-to-all-start
  16.5 0.0 all-gather.5.cloned.1.call-start
  16.5 0.0 copy-done.1
  16.5 2.5 all_gather.13
  19.0 11.4 %all_gather.14 = bf16[64,4096]{1,0:T(8,128)(2,1)} all-gather(bf16[16,4096]{1,0:T(8,128)(2,1)S(1)} %all_gather.13), channel_id=1, replica_groups=mesh['zl'=8,'x'=4,'zh'=2,'y'=4,'c'=2] {'y'}, dimensions={0}, use_global_device_ids=true | all-gather | bytes 655360 | tf_op jit(solution)/shard_map/all_gather | solution.py:22
  30.4 0.0 all-gather.5.cloned.1.call-update
  30.4 0.0 all-gather.3.cloned.1.call-start
  30.5 8.6 %all-to-all-done = bf16[4,2,896,128]{2,3,1,0:T(8,128)(2,1)S(1)} async-done(((bf16[4,2,896,128]{2,3,1,0:T(8,128)(2,1)}), bf16[4,2,896,128]{2,3,1,0:T(8,128)(2,1)S(1)}, u32[]{:S(2)}, u32[]{:S(2)}) %all-to-all-start) | async-done | bytes 1835040 | tf_op jit(solution)/shard_map/all_to_all | solution.py:33
  39.1 1.4 copy.31
  40.5 0.0 all-gather.3.cloned.1.call-update
  40.6 68.8 %all-gather.5.cloned.1.call-done = bf16[128,4096]{1,0:T(8,128)(2,1)} async-done(((bf16[64,4096]{1,0:T(8,128)(2,1)}), bf16[128,4096]{1,0:T(8,128)(2,1)}) %all-gather.5.cloned.1.call-update) | async-done | bytes 1048592 | tf_op jit(solution)/shard_map/all_gather | solution.py:23
  109.3 2.3 copy.32
  111.6 7.1 %all-to-all-start.1 = ((bf16[128,32,128]{0,2,1:T(8,128)(2,1)}), bf16[128,32,128]{0,2,1:T(8,128)(2,1)S(1)}, u32[]{:S(2)}, u32[]{:S(2)}) async-start(bf16[128,32,128]{0,2,1:T(8,128)(2,1)} %bitcast.8), calls=%async_computation.1 | async-start | bytes 2097152 | tf_op jit(solution)/shard_map/all_to_all | solution.py:29
  118.8 0.0 copy-done.2
  118.8 92.7 %all-to-all-done.1 = bf16[128,32,128]{0,2,1:T(8,128)(2,1)S(1)} async-done(((bf16[128,32,128]{0,2,1:T(8,128)(2,1)}), bf16[128,32,128]{0,2,1:T(8,128)(2,1)S(1)}, u32[]{:S(2)}, u32[]{:S(2)}) %all-to-all-start.1) | async-done | bytes 1048608 | tf_op jit(solution)/shard_map/all_to_all | solution.py:29
  211.5 0.7 copy.33
  212.2 0.0 copy-start
  212.2 0.0 copy-start.3
  212.2 0.0 copy-start.4
  212.2 231.0 %all-gather.3.cloned.1.call-done = bf16[2,896,4096]{1,2,0:T(8,128)(2,1)} async-done(((bf16[2,896,512]{1,2,0:T(8,128)(2,1)}), bf16[2,896,4096]{1,2,0:T(8,128)(2,1)}) %all-gather.3.cloned.1.call-update) | async-done | bytes 14680080 | tf_op jit(solution)/shard_map/all_gather | solution.py:35
  443.2 5.4 %multiply_convert_fusion = (bf16[128,896]{0,1:T(8,128)(2,1)S(1)}, bf16[128,896]{0,1:T(8,128)(2,1)S(1)}) fusion(bf16[128,896]{0,1:T(8,128)(2,1)S(1)} %copy.28, bf16[128,896]{0,1:T(8,128)(2,1)S(1)} %copy.29, bf16[128,4096]{1,0:T(8,128)(2,1)} %all-gather.5.cloned.1.call-done, bf16[2,896,4096]{1,2,0:T(8,128)(2,1)} %all-gather.3.cloned.1.call-done), kind=kOutput, calls=%fused_computation.27 | convolution fusion | flops 941359104 | bytes 9306112 | tf_op jit(solution)/shard_map/dot_general | solution.py:36
  448.7 0.8 copy.34
  449.5 0.8 copy.35
  450.4 0.0 copy-done
  450.4 0.0 copy-done.3
  450.4 0.0 copy-done.4
  450.4 6.4 %fusion.10 = (bf16[896,128]{1,0:T(8,128)(2,1)}, f32[896,128]{1,0:T(8,128)}, f32[896,128]{1,0:T(8,128)}) fusion(bf16[896,128]{1,0:T(8,128)(2,1)S(1)} %copy-done, f32[896]{0:T(1024)S(1)} %convert_multiply_fusion.5, f32[896,128]{1,0:T(8,128)S(1)} %copy-done.3, f32[896,128]{1,0:T(8,128)S(1)} %copy-done.4, bf16[4096,128]{1,0:T(8,128)(2,1)S(1)} %bitcast.31, ...), kind=kOutput, calls=%fused_computation.19 | convolution fusion | flops 941588480 | bytes 10685952 | tf_op jit(solution)/shard_map/dot_general | solution.py:39
  (1 shorter events, 0.0 us)
Async XLA Ops:
  7.2 9.3 %copy-start.1 = (bf16[8,4096]{1,0:T(8,128)(2,1)S(1)}, bf16[8,4096]{1,0:T(8,128)(2,1)}, u32[]{:S(2)}) copy-start(bf16[8,4096]{1,0:T(8,128)(2,1)} %param.7) | copy-start | bytes 196612
  12.3 106.4 %copy-start.2 = (s32[896]{0:T(1024)S(1)}, s32[896]{0:T(1024)}, u32[]{:S(2)}) copy-start(s32[896]{0:T(1024)} %param.13) | copy-start | bytes 10756
  12.3 26.8 %all-to-all-start = ((bf16[4,2,896,128]{2,3,1,0:T(8,128)(2,1)}), bf16[4,2,896,128]{2,3,1,0:T(8,128)(2,1)S(1)}, u32[]{:S(2)}, u32[]{:S(2)}) async-start(bf16[4,2,896,128]{2,3,1,0:T(8,128)(2,1)} %stack.19), calls=%async_computation | async-start | bytes 3670016 | tf_op jit(solution)/shard_map/all_to_all | solution.py:33
  16.5 92.9 %all-gather.5.cloned.1.call-start = ((), (), s32[]{:S(2)}) async-start(), calls=%async_computation.3 | async-start | bytes 1572864 | tf_op jit(solution)/shard_map/all_gather | solution.py:23
  30.4 412.8 %all-gather.3.cloned.1.call-start = ((), (), s32[]{:S(2)}) async-start(), calls=%async_computation.2 | async-start | bytes 16515072 | tf_op jit(solution)/shard_map/all_gather | solution.py:35
  111.6 99.9 %all-to-all-start.1 = ((bf16[128,32,128]{0,2,1:T(8,128)(2,1)}), bf16[128,32,128]{0,2,1:T(8,128)(2,1)S(1)}, u32[]{:S(2)}, u32[]{:S(2)}) async-start(bf16[128,32,128]{0,2,1:T(8,128)(2,1)} %bitcast.8), calls=%async_computation.1 | async-start | bytes 2097152 | tf_op jit(solution)/shard_map/all_to_all | solution.py:29
  212.2 238.2 %copy-start = (bf16[896,128]{1,0:T(8,128)(2,1)S(1)}, bf16[896,128]{1,0:T(8,128)(2,1)}, u32[]{:S(2)}) copy-start(bf16[896,128]{1,0:T(8,128)(2,1)} %param.10) | copy-start | bytes 688132
  212.2 238.2 %copy-start.3 = (f32[896,128]{1,0:T(8,128)S(1)}, f32[896,128]{1,0:T(8,128)}, u32[]{:S(2)}) copy-start(f32[896,128]{1,0:T(8,128)} %param.11) | copy-start | bytes 1376260
  212.2 238.2 %copy-start.4 = (f32[896,128]{1,0:T(8,128)S(1)}, f32[896,128]{1,0:T(8,128)}, u32[]{:S(2)}) copy-start(f32[896,128]{1,0:T(8,128)} %param.12) | copy-start | bytes 1376260
Sparse Core Ops, SparseCore 0:
  30.6 78.7 all-gather.4
  111.4 331.7 all-gather.2
